TPU v7x, 128 devices: a whole 4x4x4 slice. The times are simulated.
128 devices in a mesh: row: 32 (over y, x, z_hi), col: 4 (over z_lo, core).
Axes of the slice: x: 4, y: 4, z: 4 (z_hi: 2, z_lo: 2; z = z_hi * 2 + z_lo), core: 2. Of those that a mesh axis runs over, the one named last changes fastest.
Arguments:
- front_inverse: bfloat16 [24576, 24576], P('row', 'col'), may hold values from -0.0390625 to 0.0390625
- coupling_tiles: bfloat16 [768, 128, 128], P('col'), may hold values from -12 to 12
- tile_row: int32 [768], P('col'), may hold values from 0 to 191, as said below
- tile_col: int32 [768], P('col'), may hold values from 0 to 15
- surface_map: int32 [2, 8192], P(None, 'row'), may hold values from 0 to 24575, as said below
- bem_entries: bfloat16 [2, 8192, 2048], P(None, 'row', 'col'), may hold values from -6 to 6
- pivot_inverse: bfloat16 [8192, 8192], P('row'), may hold values from -0.0625 to 0.0625
- slab_below: bfloat16 [8192, 8192], P('row'), may hold values from -0.0625 to 0.0625
Outputs:
- panel_out: bfloat16 [2, 8192, 2048], P(None, 'row', 'col')
Inputs may be any that keep to these rules, and one draw needn't show every extreme that they name: `tile_row`: tiles at positions c * 192 to (c + 1) * 192 - 1 lie in block rows c * 48 to (c + 1) * 48 - 1; no two tiles share both block row and block column. `surface_map`: all entries differ; of the entries in the columns of one index of row, at most 24 lie in any one block of 768 front rows that starts at a multiple of 768, and for every index of row some block holds exactly 24 of them.
All inputs are finite; a program needn't handle non-finite values.
Results may differ from a plain program's by a relative error of at most 0.0058.
Values may be sent and summed in bfloat16 or wider, within the bound.
A program may use at most 192 MiB of HBM per device.

v0:
```python
import jax
import jax.numpy as jnp
from jax import lax
from jax.sharding import PartitionSpec as P

COLS = 2048


def fold_with(matrix, shard_piece):
    return jnp.dot(matrix, shard_piece, preferred_element_type=jnp.float32)


def per_device(
    front_inverse,
    coupling_tiles,
    tile_row,
    tile_col,
    surface_map,
    bem_entries,
    pivot_inverse,
    slab_below,
):
    row_width = front_inverse.shape[0]
    front_width = front_inverse.shape[1]
    block_count = front_width // 128
    col_blocks = COLS // 128
    tile_count = coupling_tiles.shape[0]
    group_size = min(48, tile_count)
    group_count = tile_count // group_size
    local_rows = tile_row - lax.axis_index("col") * block_count
    blocks_view = front_inverse.reshape(row_width, block_count, 128)
    block_ids = jnp.arange(col_blocks, dtype=jnp.int32)

    def group_step(total, inputs):
        tiles, rows_here, cols_here = inputs
        picked = jnp.take(blocks_view, rows_here, axis=1)
        products = jnp.einsum("tkn,rtk->tnr", tiles, picked, preferred_element_type=jnp.float32)
        placing = (cols_here[:, None] == block_ids[None, :]).astype(jnp.float32)
        placed = jnp.einsum("tb,tnr->bnr", placing, products, precision=lax.Precision.HIGHEST)
        return (total + placed.reshape(COLS, row_width), None)

    grouped = (
        coupling_tiles.reshape(group_count, group_size, 128, 128),
        local_rows.reshape(group_count, group_size),
        tile_col.reshape(group_count, group_size),
    )
    partial_all, _ = lax.scan(group_step, jnp.zeros((COLS, row_width), jnp.float32), grouped)
    col_width = COLS // lax.axis_size("col")
    complete = lax.psum(partial_all, "col")
    mine = lax.dynamic_slice_in_dim(complete, lax.axis_index("col") * col_width, col_width, 0)
    solved = mine.astype(jnp.bfloat16)
    pivot_count = surface_map.shape[1]
    initial = jnp.zeros((col_width, 2, pivot_count), jnp.bfloat16)
    shard_piece = lax.all_gather(solved, "row", axis=1, tiled=True)
    width = shard_piece.shape[1]
    inside = (surface_map >= 0) & (surface_map < width)
    taken = jnp.take(shard_piece, jnp.clip(surface_map, 0, width - 1), axis=1)
    schur_part = jnp.where(inside[None], taken, initial)
    schur_part = schur_part.transpose(1, 2, 0)
    assembled = (bem_entries.astype(jnp.float32) - schur_part.astype(jnp.float32)).astype(
        jnp.bfloat16
    )
    pivot_solved = fold_with(pivot_inverse, lax.all_gather(assembled[0], "row", axis=0, tiled=True))
    pivot_solved = pivot_solved.astype(jnp.bfloat16)
    update = fold_with(slab_below, lax.all_gather(pivot_solved, "row", axis=0, tiled=True))
    below = (assembled[1].astype(jnp.float32) - update).astype(jnp.bfloat16)
    return jnp.stack([pivot_solved, below])


def solution(mesh):
    placed = (
        P("row", "col"),
        P("col", None, None),
        P("col"),
        P("col"),
        P(None, "row"),
        P(None, "row", "col"),
        P("row", None),
        P("row", None),
    )
    return jax.shard_map(
        per_device, mesh=mesh, in_specs=placed, out_specs=P(None, "row", "col"), check_vma=False
    )
```

profile of v0, /device:TPU:0, one launch (start us, length us, event | category | flops | bytes accessed | tf_op | source)
XLA Modules:
  0.0 920.7 jit_solution(17501787212766314948)
XLA Ops:
  6.5 0.0 all-gather.5.cloned.1.call-start
  6.5 0.7 broadcast_subtract_fusion
  7.2 0.1 reshape.62
  7.3 12.7 %copy.21 = bf16[768,6144]{0,1:T(8,128)(2,1)} copy(bf16[768,6144]{1,0:T(8,128)(2,1)} %param.10) | data formatting | bytes 18874368 | tf_op args[0]
  20.0 12.7 %copy.22 = bf16[768,48,128]{2,0,1:T(8,128)(2,1)} copy(bf16[768,48,128]{0,2,1:T(8,128)(2,1)} %bitcast.67) | data formatting | bytes 18874368
  32.7 0.0 copy-start.2
  32.7 8.7 copy.20
  41.4 0.0 copy-done.2
  41.4 0.1 reshape.60
  41.5 253.7 %while.11 = (s32[]{:T(128)}, f32[2048,768]{1,0:T(8,128)}, s32[4,48]{1,0:T(4,128)S(1)}, bf16[4,48,128,128]{2,3,1,0:T(8,128)(2,1)}, s32[4,48]{1,0:T(4,128)S(1)}, /...) while((s32[]{:T(128)}, f32[2048,768]{1,0:T(8,128)}, s32[4,48]{1,0:T(4,128)S(1)}, ...), condition=%wide.region_1.2_spmd.clone, body=%wide.region_0.1_spmd.clone.sunk | while | flops 2121795712 | bytes 105388232 | solution.py:47
  41.5 10.2 %gather_fusion = bf16[48,768,128]{2,1,0:T(8,128)(2,1)} fusion(bf16[768,48,128]{2,0,1:T(8,128)(2,1)} %get-tuple-element.144, s32[1024]{0:T(1024)S(1)} %pad_clamp_fusion.3), kind=kCustom, calls=%fused_computation.clone.clone.1 | custom fusion | bytes 18874560 | tf_op jit(solution)/shard_map/while/body/eval_jaxpr/jit(_take)/gather | solution.py:36
  51.7 13.3 %fusion.44 = f32[48,128,768]{2,1,0:T(8,128)} fusion(bf16[48,768,128]{2,1,0:T(8,128)(2,1)} %gather_fusion, pred[48]{0:T(512)(128)(4,1)S(1)} %compare_and_fusion.4, bf16[4,48,128,128]{2,3,1,0:T(8,128)(2,1)} %get-tuple-element.142, s32[]{:T(128)} %get-tuple-element.131), kind=kOutput, calls=%fused_computation.5.clone.1 | convolution fusion | flops 1212678144 | bytes 29884976 | tf_op jit(solution)/shard_map/while/body/eval_jaxpr/tkn,rtk->tnr/dot_general | solution.py:37
  65.0 26.0 %fusion.46 = f32[16,128,768]{2,0,1:T(8,128)S(1)} fusion(f32[48,128,768]{2,1,0:T(8,128)} %fusion.44, s32[48]{0:T(128)S(1)} %fusion.45), kind=kOutput, calls=%fused_computation.3.clone.1 | convolution fusion | flops 905970432 | bytes 25166016 | tf_op jit(solution)/shard_map/while/body/eval_jaxpr/tb,tnr->bnr/dot_general | solution.py:39
  91.0 6.3 copy.32
  97.3 6.2 bitcast_add_fusion.2
  103.5 10.2 %gather_fusion = bf16[48,768,128]{2,1,0:T(8,128)(2,1)} fusion(bf16[768,48,128]{2,0,1:T(8,128)(2,1)} %get-tuple-element.144, s32[1024]{0:T(1024)S(1)} %pad_clamp_fusion.3), kind=kCustom, calls=%fused_computation.clone.clone.1 | custom fusion | bytes 18874560 | tf_op jit(solution)/shard_map/while/body/eval_jaxpr/jit(_take)/gather | solution.py:36
  113.6 13.3 %fusion.44 = f32[48,128,768]{2,1,0:T(8,128)} fusion(bf16[48,768,128]{2,1,0:T(8,128)(2,1)} %gather_fusion, pred[48]{0:T(512)(128)(4,1)S(1)} %compare_and_fusion.4, bf16[4,48,128,128]{2,3,1,0:T(8,128)(2,1)} %get-tuple-element.142, s32[]{:T(128)} %get-tuple-element.131), kind=kOutput, calls=%fused_computation.5.clone.1 | convolution fusion | flops 1212678144 | bytes 29884976 | tf_op jit(solution)/shard_map/while/body/eval_jaxpr/tkn,rtk->tnr/dot_general | solution.py:37
  127.0 26.0 %fusion.46 = f32[16,128,768]{2,0,1:T(8,128)S(1)} fusion(f32[48,128,768]{2,1,0:T(8,128)} %fusion.44, s32[48]{0:T(128)S(1)} %fusion.45), kind=kOutput, calls=%fused_computation.3.clone.1 | convolution fusion | flops 905970432 | bytes 25166016 | tf_op jit(solution)/shard_map/while/body/eval_jaxpr/tb,tnr->bnr/dot_general | solution.py:39
  153.0 6.3 copy.32
  159.3 8.1 bitcast_add_fusion.2
  167.4 10.1 %gather_fusion = bf16[48,768,128]{2,1,0:T(8,128)(2,1)} fusion(bf16[768,48,128]{2,0,1:T(8,128)(2,1)} %get-tuple-element.144, s32[1024]{0:T(1024)S(1)} %pad_clamp_fusion.3), kind=kCustom, calls=%fused_computation.clone.clone.1 | custom fusion | bytes 18874560 | tf_op jit(solution)/shard_map/while/body/eval_jaxpr/jit(_take)/gather | solution.py:36
  177.6 13.3 %fusion.44 = f32[48,128,768]{2,1,0:T(8,128)} fusion(bf16[48,768,128]{2,1,0:T(8,128)(2,1)} %gather_fusion, pred[48]{0:T(512)(128)(4,1)S(1)} %compare_and_fusion.4, bf16[4,48,128,128]{2,3,1,0:T(8,128)(2,1)} %get-tuple-element.142, s32[]{:T(128)} %get-tuple-element.131), kind=kOutput, calls=%fused_computation.5.clone.1 | convolution fusion | flops 1212678144 | bytes 29884976 | tf_op jit(solution)/shard_map/while/body/eval_jaxpr/tkn,rtk->tnr/dot_general | solution.py:37
  190.9 26.0 %fusion.46 = f32[16,128,768]{2,0,1:T(8,128)S(1)} fusion(f32[48,128,768]{2,1,0:T(8,128)} %fusion.44, s32[48]{0:T(128)S(1)} %fusion.45), kind=kOutput, calls=%fused_computation.3.clone.1 | convolution fusion | flops 905970432 | bytes 25166016 | tf_op jit(solution)/shard_map/while/body/eval_jaxpr/tb,tnr->bnr/dot_general | solution.py:39
  216.9 6.3 copy.32
  223.2 8.1 bitcast_add_fusion.2
  231.3 10.2 %gather_fusion = bf16[48,768,128]{2,1,0:T(8,128)(2,1)} fusion(bf16[768,48,128]{2,0,1:T(8,128)(2,1)} %get-tuple-element.144, s32[1024]{0:T(1024)S(1)} %pad_clamp_fusion.3), kind=kCustom, calls=%fused_computation.clone.clone.1 | custom fusion | bytes 18874560 | tf_op jit(solution)/shard_map/while/body/eval_jaxpr/jit(_take)/gather | solution.py:36
  241.5 13.3 %fusion.44 = f32[48,128,768]{2,1,0:T(8,128)} fusion(bf16[48,768,128]{2,1,0:T(8,128)(2,1)} %gather_fusion, pred[48]{0:T(512)(128)(4,1)S(1)} %compare_and_fusion.4, bf16[4,48,128,128]{2,3,1,0:T(8,128)(2,1)} %get-tuple-element.142, s32[]{:T(128)} %get-tuple-element.131), kind=kOutput, calls=%fused_computation.5.clone.1 | convolution fusion | flops 1212678144 | bytes 29884976 | tf_op jit(solution)/shard_map/while/body/eval_jaxpr/tkn,rtk->tnr/dot_general | solution.py:37
  254.8 26.0 %fusion.46 = f32[16,128,768]{2,0,1:T(8,128)S(1)} fusion(f32[48,128,768]{2,1,0:T(8,128)} %fusion.44, s32[48]{0:T(128)S(1)} %fusion.45), kind=kOutput, calls=%fused_computation.3.clone.1 | convolution fusion | flops 905970432 | bytes 25166016 | tf_op jit(solution)/shard_map/while/body/eval_jaxpr/tb,tnr->bnr/dot_general | solution.py:39
  280.8 6.3 copy.32
  287.1 8.1 bitcast_add_fusion.2
  295.2 6.6 copy.23
  301.8 0.0 copy-start.1
  301.8 112.9 %all-reduce.1 = bf16[2048,768]{0,1:T(8,128)(2,1)S(1)} all-reduce(f32[2048,768]{0,1:T(8,128)} %copy.23), channel_id=1, replica_groups=mesh['row'=32,'col'=4] {'col'}, use_global_device_ids=true, to_apply=%region_2.3 | all-reduce | flops 1572864 | bytes 9437184 | tf_op jit(solution)/shard_map/psum | solution.py:49
  414.7 1.0 dynamic-slice_convert_fusion
  415.7 0.0 all-gather.5.cloned.1.call-update
  415.8 0.0 all-gather.9.cloned.1.call-start
  415.8 0.0 copy-done.1
  415.9 1.2 copy.19
  417.1 209.3 %all-gather.5.cloned.1.call-done = bf16[512,24576]{0,1:T(8,128)(2,1)} async-done(((bf16[512,768]{0,1:T(8,128)(2,1)}), bf16[512,24576]{0,1:T(8,128)(2,1)}) %all-gather.5.cloned.1.call-update) | async-done | bytes 25165840 | tf_op jit(solution)/shard_map/all_gather | solution.py:54
  626.5 13.4 %gather_fusion.1 = bf16[512,512]{1,0:T(8,128)(2,1)S(1)} fusion(bf16[512,24576]{0,1:T(8,128)(2,1)} %all-gather.5.cloned.1.call-done, s32[1024]{0:T(1024)S(1)} %pad_clamp_fusion.1), kind=kCustom, calls=%fused_computation.1 | custom fusion | bytes 1050624 | tf_op jit(solution)/shard_map/jit(_take)/gather | solution.py:57
  639.8 0.2 copy.24
  640.0 0.2 fusion.26
  640.3 0.7 slice.12
  641.0 0.0 all-gather.9.cloned.1.call-update
  641.0 0.0 all-gather.7.cloned.1.call-start
  641.1 129.2 %all-gather.9.cloned.1.call-done = bf16[1,8192,512]{1,2,0:T(8,128)(2,1)} async-done(((bf16[1,256,512]{1,2,0:T(8,128)(2,1)}), bf16[1,8192,512]{1,2,0:T(8,128)(2,1)}) %all-gather.9.cloned.1.call-update) | async-done | bytes 8388624 | tf_op jit(solution)/shard_map/all_gather | solution.py:63
  770.2 7.6 fusion.22
  777.8 0.0 all-gather.7.cloned.1.call-update
  777.9 0.0 copy-start
  777.9 128.3 %all-gather.7.cloned.1.call-done = bf16[8192,512]{0,1:T(8,128)(2,1)} async-done(((bf16[256,512]{0,1:T(8,128)(2,1)}), bf16[8192,512]{0,1:T(8,128)(2,1)}) %all-gather.7.cloned.1.call-update) | async-done | bytes 8388624 | tf_op jit(solution)/shard_map/all_gather | solution.py:65
  906.2 6.9 fusion.25
  913.1 0.0 copy-done
  913.1 0.1 pad_maximum_fusion
  913.2 1.0 copy.25
  (21 shorter events, 0.1 us)
Async XLA Ops:
  6.5 619.9 %all-gather.5.cloned.1.call-start = ((), (), s32[]{:S(2)}) async-start(), calls=%async_computation | async-start | bytes 25952256 | tf_op jit(solution)/shard_map/all_gather | solution.py:54
  32.7 8.7 copy-start.2
  301.8 114.0 %copy-start.1 = (s32[2,256]{1,0:T(2,128)S(1)}, s32[2,256]{1,0:T(2,128)}, u32[]{:S(2)}) copy-start(s32[2,256]{1,0:T(2,128)} %param.14) | copy-start | bytes 6148
  415.8 354.4 %all-gather.9.cloned.1.call-start = ((), (), s32[]{:S(2)}) async-start(), calls=%async_computation.2 | async-start | bytes 8650752 | tf_op jit(solution)/shard_map/all_gather | solution.py:63
  641.0 265.2 %all-gather.7.cloned.1.call-start = ((), (), s32[]{:S(2)}) async-start(), calls=%async_computation.1 | async-start | bytes 8650752 | tf_op jit(solution)/shard_map/all_gather | solution.py:65
  777.9 135.2 %copy-start = (bf16[512,256]{1,0:T(8,128)(2,1)S(1)}, bf16[512,256]{1,0:T(8,128)(2,1)}, u32[]{:S(2)}) copy-start(bf16[512,256]{1,0:T(8,128)(2,1)} %fusion.22) | copy-start | bytes 786436
Sparse Core Ops, SparseCore 0:
  415.9 210.5 all-gather.4
  641.1 129.0 all-gather.8
  778.0 128.1 all-gather.6
where the time goes:
time: 922 us; the launch traced here: 921 us
  waiting for transfers between devices  467 us (51%)
  matrix products  172 us (19%)
  local copies, waits for them, and re-layouts  124 us (13%)
  blocking collectives  113 us (12%)
  other arithmetic  31.6 us (3%)
  between operations  13.2 us (1%)
    all_gather x1, waiting for transfers between devices, per_device(): shard_piece = lax.all_gather(solved, 'row', axis=1, tiled=True)  209 us
    all_gather x1, waiting for transfers between devices, per_device(): lax.all_gather(assembled[0], 'row', axis=0, tiled=True)  129 us
    all_gather x1, waiting for transfers between devices, per_device(): lax.all_gather(pivot_solved, 'row', axis=0, tiled=True)  128 us
    psum x1, blocking collectives, per_device(): complete = lax.psum(partial_all, 'col')  113 us
    dot_general x4, matrix products, group_step(): jnp.einsum('tb,tnr->bnr', placing, products, precision=lax.Precision.HIGH...  104 us
    dot_general x4, matrix products, group_step(): jnp.einsum('tkn,rtk->tnr', tiles, picked, preferred_element_type=jnp.floa...  53.4 us
    gather x4, local copies, waits for them, and re-layouts, group_step(): picked = jnp.take(blocks_view, rows_here, axis=1)  40.6 us
    unnamed x11, local copies, waits for them, and re-layouts  35.3 us
  transfers between devices with their start and end apart: 3, of which 3 were waited for; matrix products, arithmetic and copies ran while one was open for 0% of the time, Pallas kernels for 0%

commit v1 on v0

v1 whole, which is shorter than its diff:
```python
import functools
import heapq

import jax
import jax.numpy as jnp
from jax import lax
from jax.experimental import pallas as pl
from jax.experimental.pallas import tpu as pltpu
from jax.sharding import PartitionSpec as P

MESH = pl.DeviceIdType.MESH
F32, BF16, I32 = jnp.float32, jnp.bfloat16, jnp.int32
N_ROW, CAP = 32, 24
SLOTS = N_ROW * CAP
ROWS = 768
GROUP = 4
TILES = 192
CHUNKS = (TILES + 16 * (GROUP - 1)) // GROUP
UNROLL = 2


def front_kernel(trow, tcol, f_hbm, t_hbm, out_hbm, f, w, acc, ob, lrs, ccol, pos, cnt, fsem, tsem, osem):
    load = pltpu.make_async_copy(f_hbm, f, fsem)
    load.start()
    first = lax.axis_index("col") * 48
    chunks = w.shape[0]

    @pl.loop(0, 16)
    def _(b):
        cnt[b] = 0

    @pl.loop(0, TILES)
    def _(i):
        b = tcol[i]
        cnt[b] = cnt[b] + 1

    def place(b, at):
        n = cnt[b]
        used = (n + GROUP - 1) // GROUP
        pos[b] = at * GROUP

        def name(c, _):
            ccol[at + c] = b
            return 0

        lax.fori_loop(0, used, name, 0)

        def clear(s, _):
            lrs[s] = 0
            w[s // GROUP, pl.ds(pl.multiple_of((s % GROUP) * 128, 128), 128), :] = jnp.zeros((128, 128), BF16)
            return 0

        lax.fori_loop(at * GROUP + n, (at + used) * GROUP, clear, 0)
        return at + used

    total = lax.fori_loop(0, 16, place, 0)

    @pl.loop(0, TILES)
    def _(i):
        b = tcol[i]
        s = pos[b]
        pos[b] = s + 1
        lrs[s] = trow[i] - first
        pltpu.make_async_copy(
            t_hbm.at[i], w.at[s // GROUP, pl.ds(pl.multiple_of((s % GROUP) * 128, 128), 128), :], tsem
        ).start()

    acc[...] = jnp.zeros_like(acc)

    @pl.when(total % UNROLL != 0)
    def _():
        ccol[total] = 0
        for g in range(GROUP):
            lrs[total * GROUP + g] = 0
        w[total] = jnp.zeros((GROUP * 128, 128), BF16)

    @pl.loop(0, TILES)
    def _(i):
        pltpu.make_async_copy(t_hbm.at[0], w.at[0, pl.ds(0, 128), :], tsem).wait()

    load.wait()

    @pl.loop(0, (total + UNROLL - 1) // UNROLL)
    def _(it):
        for u in range(UNROLL):
            c = it * UNROLL + u
            parts = []
            for g in range(GROUP):
                lr = pl.multiple_of(lrs[c * GROUP + g] * 128, 128)
                parts.append(f[:, pl.ds(lr, 128)])
            lhs = jnp.concatenate(parts, axis=1)
            at = pl.multiple_of(ccol[c] * 128, 128)
            acc[:, pl.ds(at, 128)] += jnp.dot(lhs, w[c], preferred_element_type=F32)

    for k in range(4):
        ob[k] = acc[:, k * 512 : (k + 1) * 512].astype(BF16)
        pltpu.make_async_copy(ob.at[k], out_hbm.at[k], osem.at[k]).start()
    for k in range(4):
        pltpu.make_async_copy(ob.at[k], out_hbm.at[k], osem.at[k]).wait()


def front(trow, tcol, f, tiles):
    smem = pl.BlockSpec(memory_space=pltpu.SMEM)
    hbm = pl.BlockSpec(memory_space=pl.ANY)
    chunks = CHUNKS + CHUNKS % UNROLL
    return pl.pallas_call(
        front_kernel,
        out_shape=jax.ShapeDtypeStruct((4, ROWS, 512), BF16),
        in_specs=[smem, smem, hbm, hbm],
        out_specs=hbm,
        scratch_shapes=[
            pltpu.VMEM((ROWS, 6144), BF16),
            pltpu.VMEM((chunks, GROUP * 128, 128), BF16),
            pltpu.VMEM((ROWS, 2048), F32),
            pltpu.VMEM((4, ROWS, 512), BF16),
            pltpu.SMEM((chunks * GROUP,), I32),
            pltpu.SMEM((chunks,), I32),
            pltpu.SMEM((16,), I32),
            pltpu.SMEM((16,), I32),
            pltpu.SemaphoreType.DMA,
            pltpu.SemaphoreType.DMA,
            pltpu.SemaphoreType.DMA((4,)),
        ],
        compiler_params=pltpu.CompilerParams(vmem_limit_bytes=56 << 20),
        name="front",
    )(trow, tcol, f, tiles)


def route_kernel(
    req, slotcol, part, bem, out, x, o, of, r, reqin, cv, perm, sm, rb,
    ps, pr, rs, rr, sends, recvs,
):
    me, col = lax.axis_index("row"), lax.axis_index("col")
    q, lo = col % 2, col // 2
    barrier = pltpu.get_barrier_semaphore()

    def tell(a, b):
        pl.semaphore_signal(barrier, inc=1, device_id=(a, b), device_id_type=MESH)

    tell(me, lo * 2 + 1 - q)
    tell(me, (1 - lo) * 2 + q)

    @pl.loop(1, N_ROW)
    def _(p):
        for l in range(2):
            tell(lax.rem(me + p, N_ROW), l * 2 + q)

    pl.semaphore_wait(barrier, 64)

    def swap(l):
        return pltpu.make_async_remote_copy(
            part.at[l * 2 + 1 - q], x.at[l], ps.at[l], pr.at[l], device_id=(me, lo * 2 + 1 - q), device_id_type=MESH
        )

    def ask(s, who):
        return pltpu.make_async_remote_copy(
            req.at[s], reqin.at[who], rs.at[s], rr.at[who], device_id=(s, col), device_id_type=MESH
        )

    def give(l, d, who, wl):
        return pltpu.make_async_remote_copy(
            o.at[l, d], r.at[wl, who], sends.at[l, d], recvs.at[wl, who],
            device_id=(d, l * 2 + q), device_id_type=MESH,
        )

    swap(0).start()
    swap(1).start()

    @pl.loop(1, N_ROW)
    def _(p):
        ask(lax.rem(me + p, N_ROW), me).start()

    reqin[me] = req[me]

    @pl.loop(1, N_ROW)
    def _(p):
        s = lax.rem(me + p, N_ROW)
        ask(s, s).wait_recv()

    lane = lax.broadcasted_iota(I32, (CAP, 128), 1)
    line = lax.broadcasted_iota(I32, (CAP, 128), 0)

    @pl.loop(0, N_ROW)
    def _(d):
        row = jnp.broadcast_to(reqin[d], (CAP, 128))
        val = jnp.sum(jnp.where(lane == line, row, 0), axis=1, keepdims=True)
        cv[pl.ds(pl.multiple_of(d * CAP, 8), CAP), :] = jnp.broadcast_to(val, (CAP, 128))

    @pl.loop(0, SLOTS // 128)
    def _(b):
        at = pl.ds(pl.multiple_of(b * 128, 128), 128)
        want = cv[at, :]
        for j in range(ROWS // 128):
            here = lax.broadcasted_iota(I32, (128, 128), 1) + j * 128
            perm[at, j * 128 : (j + 1) * 128] = (want == here).astype(F32).astype(BF16)

    for l in range(2):
        swap(l).wait_recv()
        sm[...] = (part[l * 2 + q].astype(F32) + x[l].astype(F32)).astype(BF16)
        of[...] = jnp.dot(perm[...], sm[...], preferred_element_type=F32)

        @pl.loop(0, N_ROW)
        def _(d):
            o[l, d] = of[pl.ds(pl.multiple_of(d * CAP, 8), CAP), :].astype(BF16)

        @pl.loop(1, N_ROW)
        def _(p):
            give(l, lax.rem(me + p, N_ROW), me, lo).start()

    give(1 - lo, me, me, lo).start()
    r[lo, me] = o[lo, me]
    give(lo, me, me, 1 - lo).wait_recv()
    of[pl.ds(pl.multiple_of(me * CAP, 8), CAP), :] = r[0, me].astype(F32) + r[1, me].astype(F32)

    @pl.loop(1, N_ROW)
    def _(p):
        s = lax.rem(me + N_ROW - p, N_ROW)
        for l in range(2):
            give(lo, s, s, l).wait_recv()
        of[pl.ds(pl.multiple_of(s * CAP, 8), CAP), :] = r[0, s].astype(F32) + r[1, s].astype(F32)

    rb[...] = of[...].astype(BF16)
    for p in range(2):
        pick = slotcol[p * 256 : (p + 1) * 256, :]
        sel = jnp.concatenate(
            [
                (pick == lax.broadcasted_iota(I32, (256, 128), 1) + j * 128).astype(F32).astype(BF16)
                for j in range(SLOTS // 128)
            ],
            axis=1,
        )
        schur = jnp.dot(sel, rb[...], preferred_element_type=F32)
        out[p] = (bem[p].astype(F32) - schur).astype(BF16)

    for l in range(2):
        swap(l).wait_send()
    give(1 - lo, me, me, lo).wait_send()

    @pl.loop(1, N_ROW)
    def _(p):
        d = lax.rem(me + p, N_ROW)
        ask(d, me).wait_send()
        for l in range(2):
            give(l, d, me, lo).wait_send()


def route(req, slotcol, part, bem):
    vm = pl.BlockSpec(memory_space=pltpu.VMEM)
    dma = pltpu.SemaphoreType.DMA
    return pl.pallas_call(
        route_kernel,
        out_shape=jax.ShapeDtypeStruct((2, 256, 512), BF16),
        in_specs=[vm] * 4,
        out_specs=vm,
        scratch_shapes=[
            pltpu.VMEM((2, ROWS, 512), BF16),
            pltpu.VMEM((2, N_ROW, CAP, 512), BF16),
            pltpu.VMEM((SLOTS, 512), F32),
            pltpu.VMEM((2, N_ROW, CAP, 512), BF16),
            pltpu.VMEM((N_ROW, 1, 128), I32),
            pltpu.VMEM((SLOTS, 128), I32),
            pltpu.VMEM((SLOTS, ROWS), BF16),
            pltpu.VMEM((ROWS, 512), BF16),
            pltpu.VMEM((SLOTS, 512), BF16),
            dma((2,)), dma((2,)), dma((N_ROW,)), dma((N_ROW,)), dma((2, N_ROW)), dma((2, N_ROW)),
        ],
        compiler_params=pltpu.CompilerParams(collective_id=0, has_side_effects=True, vmem_limit_bytes=56 << 20),
        name="route",
    )(req, slotcol, part, bem)


def plan():
    free, heap, sends, arrivals = {}, [], [], []
    count = 0

    def send(t, item, h, stage, step):
        nonlocal count
        link = ("z", 0) if stage == 0 else ((h + stage) % 2, step)
        busy = 5.6 if stage == 0 else 2.8
        go = max(t, free.get(link, 0.0))
        free[link] = go + busy
        count += 1
        heapq.heappush(heap, (go + busy + 1.5, count, item, h, stage, step))
        return (item, h, stage, step)

    def spread(t, item, h):
        k, m, z = item
        out = []
        if m == 0 and k == 0:
            out += [send(t, item, h, 1, s) for s in ((1, -1) if z == 0 else (-1, 1))]
        if m == 0:
            out += [send(t, item, h, 2, s) for s in ((1, -1) if (k + z) % 2 == 0 else (-1, 1))]
        return out

    start = []
    for h in range(2):
        start.append(send(0.0, (0, 0, 0), h, 0, 0))
    first = [spread(0.0, (0, 0, 0), h) for h in range(2)]
    for a, b in zip(*first):
        start += [a, b]
    while heap:
        t, _, (k, m, z), h, stage, step = heapq.heappop(heap)
        out = []
        if stage == 0:
            item = (0, 0, 1)
        elif stage == 1:
            item = ((k - step + 1) % 4 - 1 if k - step != -2 else 2, 0, z)
            if k == 0 and step == (1 if z == 0 else -1):
                out.append(send(t, item, h, 1, step))
        else:
            item = (k, (m - step + 1) % 4 - 1 if m - step != -2 else 2, z)
            if m == 0 and step == (1 if (k + z) % 2 == 0 else -1):
                out.append(send(t, item, h, 2, step))
        out += spread(t, item, h)
        arrivals.append((item, h, out))
    return start, arrivals


def panel_kernel(asm, a_piv, a_low, out, a0, a1, b0, b1, acc, asem, send_sem, recv_sem):
    me, col = lax.axis_index("row"), lax.axis_index("col")
    my, mx, mz = me // 8, (me // 2) % 4, me % 2

    def slot(dy, dx, dz):
        return (((my + dy + 4) % 4) * 4 + (mx + dx + 4) % 4) * 2 + (mz + dz) % 2

    loads = [pltpu.make_async_copy(a_piv, a0, asem.at[0]), pltpu.make_async_copy(a_low, a1, asem.at[1])]
    for load in loads:
        load.start()
    barrier = pltpu.get_barrier_semaphore()
    for d in ((1, 0, 0), (-1, 0, 0), (0, 1, 0), (0, -1, 0), (0, 0, 1)):
        pl.semaphore_signal(barrier, inc=1, device_id=(slot(*d), col), device_id_type=MESH)

    def at(item, h):
        k, m, z = item
        return slot(m, k, z) if h == 0 else slot(k, m, z)

    start, arrivals = plan()

    def gather(phase, a, b, load):
        sent = []

        def go(one):
            item, h, stage, step = one
            where = at(item, h)
            if stage == 0:
                to = slot(0, 0, 1)
            elif (h + stage) % 2 == 1:
                to = slot(0, step, 0)
            else:
                to = slot(step, 0, 0)
            copy = pltpu.make_async_remote_copy(
                b.at[where, h], b.at[where, h], send_sem.at[phase, len(sent)], recv_sem.at[phase, where, h],
                device_id=(to, col), device_id_type=MESH,
            )
            copy.start()
            sent.append(copy)

        def product(pair):
            cols = [a[:, pl.ds(pl.multiple_of(at(i, h) * 256 + h * 128, 128), 128)] for i, h in pair]
            rows = [b[at(i, h), h] for i, h in pair]
            return jnp.dot(jnp.concatenate(cols, axis=1), jnp.concatenate(rows, axis=0), preferred_element_type=F32)

        for one in start:
            go(one)
        load.wait()
        acc[...] = product([((0, 0, 0), 0), ((0, 0, 0), 1)])
        held = []
        for item, h, out_sends in arrivals:
            where = at(item, h)
            pltpu.make_async_remote_copy(
                b.at[where, h], b.at[where, h], send_sem.at[phase, 0], recv_sem.at[phase, where, h],
                device_id=(me, col), device_id_type=MESH,
            ).wait_recv()
            for one in out_sends:
                go(one)
            held.append((item, h))
            if len(held) == 2:
                acc[...] += product(held)
                held = []
        return sent

    b0[me, 0] = asm[0, :128, :]
    b0[me, 1] = asm[0, 128:, :]
    pl.semaphore_wait(barrier, 5)
    sent = gather(0, a0, b0, loads[0])
    solved = acc[...].astype(BF16)
    b1[me, 0] = solved[:128]
    b1[me, 1] = solved[128:]
    out[0] = solved
    sent += gather(1, a1, b1, loads[1])
    out[1] = (asm[1].astype(F32) - acc[...]).astype(BF16)
    for copy in sent:
        copy.wait_send()


def panel(asm, a_piv, a_low):
    vm = pl.BlockSpec(memory_space=pltpu.VMEM)
    hbm = pl.BlockSpec(memory_space=pl.ANY)
    dma = pltpu.SemaphoreType.DMA
    start, arrivals = plan()
    sends = len(start) + sum(len(a[2]) for a in arrivals)
    return pl.pallas_call(
        panel_kernel,
        out_shape=jax.ShapeDtypeStruct((2, 256, 512), BF16),
        in_specs=[vm, hbm, hbm],
        out_specs=vm,
        scratch_shapes=[
            pltpu.VMEM((256, 8192), BF16),
            pltpu.VMEM((256, 8192), BF16),
            pltpu.VMEM((N_ROW, 2, 128, 512), BF16),
            pltpu.VMEM((N_ROW, 2, 128, 512), BF16),
            pltpu.VMEM((256, 512), F32),
            dma((2,)), dma((2, sends)), dma((2, N_ROW, 2)),
        ],
        compiler_params=pltpu.CompilerParams(collective_id=1, has_side_effects=True, vmem_limit_bytes=56 << 20),
        name="panel",
    )(asm, a_piv, a_low)


def routes(surface_map):
    flat = surface_map.reshape(-1)
    owner, local = flat // ROWS, flat % ROWS
    n = flat.shape[0]
    ids = jnp.arange(n, dtype=I32)
    before = (owner[:, None] == owner[None, :]) & (ids[None, :] < ids[:, None])
    slot = owner * CAP + jnp.sum(before.astype(I32), axis=1)
    want = jnp.arange(N_ROW * 128, dtype=I32)
    at = jnp.where(want % 128 < CAP, (want // 128) * CAP + want % 128, -1)
    hit = at[:, None] == slot[None, :]
    req = jnp.sum(jnp.where(hit, local[None, :] + 1, 0), axis=1) - 1
    return req.reshape(N_ROW, 1, 128), jnp.broadcast_to(slot[:, None], (n, 128))


def per_device(front_inverse, tiles, tile_row, tile_col, surface_map, bem, pivot, below):
    req, slotcol = routes(surface_map)
    part = front(tile_row, tile_col, front_inverse, tiles)
    asm = route(req, slotcol, part, bem)
    return panel(asm, pivot, below)


def solution(mesh):
    placed = (
        P("row", "col"),
        P("col", None, None),
        P("col"),
        P("col"),
        P(None, "row"),
        P(None, "row", "col"),
        P("row", None),
        P("row", None),
    )
    return jax.shard_map(
        per_device, mesh=mesh, in_specs=placed, out_specs=P(None, "row", "col"), check_vma=False
    )
```

time: 922 us -> 190 us (0.21)
  waiting for transfers between devices: 467 us -> 0 us
  Pallas kernels: 0 us -> 183 us
  matrix products: 172 us -> 0 us
  local copies, waits for them, and re-layouts: 124 us -> 2.73 us
  blocking collectives: 113 us -> 0 us
  other arithmetic: 31.6 us -> 3.64 us
  between operations: 13.2 us -> 0.05 us
    all_gather x3 -> x0, waiting for transfers between devices: 467 us -> none  [the longest x1 209 us: per_device(): shard_piece = lax.all_gather(solved, 'row', axis=1, tiled=True)]
    pallas_call x0 -> x3, Pallas kernels: none -> 183 us  [the longest x1 106 us: panel(): pl.pallas_call(panel_kernel, out_shape=jax.ShapeDtypeStruct((2, 256, 512)...]
    dot_general x10 -> x0, matrix products: 172 us -> none  [the longest x4 104 us: group_step(): jnp.einsum('tb,tnr->bnr', placing, products, precision=lax.Precision.HIGH...]
    psum x1 -> x0, blocking collectives: 113 us -> none  [per_device(): complete = lax.psum(partial_all, 'col')]
    gather x6 -> x0, local copies, waits for them, and re-layouts: 54.2 us -> none  [the longest x4 40.6 us: group_step(): picked = jnp.take(blocks_view, rows_here, axis=1)]
    unnamed x11 -> x3, local copies, waits for them, and re-layouts: 35.3 us -> 1.87 us
    add x4 -> x1, other arithmetic: 30.5 us -> 0.01 us  [routes(): slot = owner * CAP + jnp.sum(before.astype(I32), axis=1)]
    dot_general x4 -> x0, local copies, waits for them, and re-layouts: 25.1 us -> none  [group_step(): jnp.einsum('tb,tnr->bnr', placing, products, precision=lax.Precision.HIGH...]
  transfers between devices with their start and end apart: 3 -> 0, of which waited for: 3 -> 0; matrix products, arithmetic and copies ran while one was open for 0% -> 0% of each run, Pallas kernels for 0% -> 0%
where the time goes in v1:
time: 190 us
  Pallas kernels  183 us (96%)
  other arithmetic  3.64 us (2%)
  local copies, waits for them, and re-layouts  2.73 us (1%)
    pallas_call x1, Pallas kernels, panel(): pl.pallas_call(panel_kernel, out_shape=jax.ShapeDtypeStruct((2, 256, 512)...  106 us
    pallas_call x1, Pallas kernels, route(): pl.pallas_call(route_kernel, out_shape=jax.ShapeDtypeStruct((2, 256, 512)...  49.8 us
    pallas_call x1, Pallas kernels, front(): pl.pallas_call(front_kernel, out_shape=jax.ShapeDtypeStruct((4, ROWS, 512...  27.3 us

profile of v1, /device:TPU:0, one launch (start us, length us, event | category | flops | bytes accessed | tf_op | source)
XLA Modules:
  0.0 189.6 jit_solution(5138891132687520910)
XLA Ops:
  0.0 0.7 sign_compare_fusion
  0.7 0.7 divide_bitcast_fusion
  1.4 0.2 convert_reduce_fusion
  1.7 1.4 select_reduce_fusion
  3.1 0.6 broadcast_add_fusion
  3.7 0.8 broadcast_in_dim.18.slotcol
  4.5 27.3 %front.1.part = bf16[4,768,512]{2,1,0:T(8,128)(2,1)} custom-call(s32[192]{0:T(256)} %trow.1, s32[192]{0:T(256)} %tcol.1, bf16[768,6144]{1,0:T(8,128)(2,1)} %f_hbm.1, bf16[192,128,128]{2,1,0:T(8,128)(2,1)} %t_hbm.1), custom_call_target="tpu_custom_call" | custom-call | tf_op jit(solution)/shard_map/front/pallas_call | solution.py:106
  31.8 49.8 %route.1.asm = bf16[2,256,512]{2,1,0:T(8,128)(2,1)} custom-call(s32[32,1,128]{2,1,0:T(1,128)} %bitcast.7, s32[512,128]{1,0:T(8,128)} %broadcast_in_dim.18.slotcol, bf16[4,768,512]{2,1,0:T(8,128)(2,1)} %front.1.part, bf16[2,256,512]{2,1,0:T(8,128)(2,1)} %bem.1), custom_call_target="tpu_custom_call" | custom-call | tf_op jit(solution)/shard_map/route/pallas_call | solution.py:250
  81.6 106.1 %panel.1 = bf16[2,256,512]{2,1,0:T(8,128)(2,1)} custom-call(bf16[2,256,512]{2,1,0:T(8,128)(2,1)} %route.1.asm, bf16[256,8192]{1,0:T(8,128)(2,1)} %a_piv.1, bf16[256,8192]{1,0:T(8,128)(2,1)} %a_low.1), custom_call_target="tpu_custom_call" | custom-call | tf_op jit(solution)/shard_map/panel/pallas_call | solution.py:402
  187.7 1.9 copy.12
  (6 shorter events, 0.0 us)
